TPU v7x, 32 devices: a whole 2x2x4 slice. The times are simulated.
32 devices in a mesh: row: 4 (over z), col: 8 (over y, x, core).
Axes of the slice: x: 2, y: 2, z: 4, core: 2. Of those that a mesh axis runs over, the one named last changes fastest.
Arguments:
- trailing: float32 [16384, 3072], P('row', 'col'), may hold values from -6 to 6
- leaf_vectors: float32 [16384, 256], P(('row', 'col')), may hold values from -1 to 1, as said below
- leaf_factor: float32 [1024, 256], P(('row', 'col')), may hold values from -1 to 2, as said below
- tree_vectors: float32 [1024, 256], P(('row', 'col')), may hold values from -1 to 1, as said below
- tree_factor: float32 [1024, 256], P(('row', 'col')), may hold values from -1 to 2, as said below
Outputs:
- updated: float32 [16384, 3072], P('row', 'col')
Inputs may be any that keep to these rules, and one draw needn't show every extreme that they name: `leaf_vectors`: in each row block of 4096 rows, row r < 256 of the block holds 1 in column r and 0 in every column after r. `leaf_factor`: each 256 x 256 block is upper triangular with its diagonal between 1 and 2. `tree_vectors`: each 256 x 256 block is upper triangular. `tree_factor`: each 256 x 256 block is upper triangular with its diagonal between 1 and 2.
All inputs are finite; a program needn't handle non-finite values.
Results may differ from a plain program's by a relative error of at most 0.0002.
Values sent between devices are 32-bit elements; how exact they have to be, the bound alone decides.
No kernel may reach another device: no remote copies, remote signals or barrier semaphores. Data moves between devices by JAX's collectives and lax.ppermute only.
A program may use at most 128 MiB of HBM per device.

v0:
```python
import jax
import jax.numpy as jnp
from jax import lax
from jax.sharding import PartitionSpec as P

highest = lax.Precision.HIGHEST
contract_rows = (((0,), (0,)), ((), ()))


def swapped(array, axis, apart):
    return lax.ppermute(array, axis, [(i, i ^ 1 << apart) for i in range(lax.axis_size(axis))])


def left_product(first, second):
    return lax.dot_general(
        first, second, contract_rows, precision=highest, preferred_element_type=jnp.float32
    )


def plain_product(first, second):
    return jnp.dot(first, second, precision=highest, preferred_element_type=jnp.float32)


def shards(trailing, leaf_vectors, leaf_factor, tree_vectors, tree_factor):
    panel_width = leaf_factor.shape[1]
    panel, block_factor, own_vectors, own_factor = (
        lax.all_gather(leaf_vectors, "col", axis=0, tiled=True),
        lax.all_gather(leaf_factor, "col", axis=0, tiled=True),
        lax.all_gather(tree_vectors, "col", axis=0, tiled=True),
        lax.all_gather(tree_factor, "col", axis=0, tiled=True),
    )
    weights = left_product(block_factor, left_product(panel, trailing))
    updated = trailing - plain_product(panel, weights)
    upper_rows = updated[:panel_width]
    lower_rows = updated[panel_width:]
    sections = lax.axis_size("row").bit_length() - 1
    position = lax.axis_index("row")
    pair_vectors, pair_factor = (
        lax.all_gather(own_vectors, "row", axis=0, tiled=True),
        lax.all_gather(own_factor, "row", axis=0, tiled=True),
    )
    current = upper_rows
    final_top = upper_rows
    for level_bit in range(sections):
        stride = 1 << level_bit
        partner_top = swapped(current, "row", level_bit)
        on_upper = position // stride % 2 == 1
        lower_group = jnp.where(on_upper, partner_top, current)
        upper_group = jnp.where(on_upper, current, partner_top)
        chosen = position // (2 * stride) * (2 * stride) + stride
        vectors = lax.dynamic_slice_in_dim(pair_vectors, chosen * panel_width, panel_width, 0)
        factor = lax.dynamic_slice_in_dim(pair_factor, chosen * panel_width, panel_width, 0)
        tree_weights = left_product(factor, lower_group + left_product(vectors, upper_group))
        final_top = jnp.where(
            position % (2 * stride) == stride,
            upper_group - plain_product(vectors, tree_weights),
            final_top,
        )
        current = lower_group - tree_weights
    final_top = jnp.where(position == 0, current, final_top)
    return jnp.concatenate([final_top, lower_rows], 0)


def solution(mesh):
    placed = (
        P("row", "col"),
        P(("row", "col"), None),
        P(("row", "col"), None),
        P(("row", "col"), None),
        P(("row", "col"), None),
    )
    return jax.shard_map(
        shards, mesh=mesh, in_specs=placed, out_specs=P("row", "col"), check_vma=False
    )
```

profile of v0, /device:TPU:0, one launch (start us, length us, event | category | flops | bytes accessed | tf_op | source)
XLA Modules:
  0.0 161.5 jit_solution(10669404419144354708)
XLA Ops:
  6.5 0.0 all-gather.4.cloned.1.call-start
  6.5 0.7 all-gather.4.cloned.1.call-update
  7.3 0.0 all-gather.8.cloned.1.call-start
  7.3 12.6 %all_gather.22 = f32[256,256]{1,0:T(8,128)} all-gather(f32[32,256]{1,0:T(8,128)} %param.8), channel_id=1, replica_groups=mesh['row'=4,'col'=8] {'col'}, dimensions={0}, use_global_device_ids=true | all-gather | bytes 294912 | tf_op jit(solution)/shard_map/all_gather | solution.py:29
  19.9 0.0 all-gather.8.cloned.1.call-update
  19.9 0.0 all-gather.6.cloned.1.call-start
  20.0 10.6 %all_gather.20 = f32[256,256]{1,0:T(8,128)} all-gather(f32[32,256]{1,0:T(8,128)} %param.9), channel_id=1, replica_groups=mesh['row'=4,'col'=8] {'col'}, dimensions={0}, use_global_device_ids=true | all-gather | bytes 294912 | tf_op jit(solution)/shard_map/all_gather | solution.py:30
  30.6 0.0 all-gather.6.cloned.1.call-update
  30.6 9.8 %all_gather.19 = f32[256,256]{1,0:T(8,128)S(1)} all-gather(f32[32,256]{1,0:T(8,128)} %param.7), channel_id=1, replica_groups=mesh['row'=4,'col'=8] {'col'}, dimensions={0}, use_global_device_ids=true | all-gather | bytes 294912 | tf_op jit(solution)/shard_map/all_gather | solution.py:28
  40.4 6.6 %copy.6 = f32[4096,384]{0,1:T(8,128)} copy(f32[4096,384]{1,0:T(8,128)} %param.5) | data formatting | bytes 12582912 | tf_op args[0]
  47.0 3.2 %all-gather.4.cloned.1.call-done = f32[4096,256]{1,0:T(8,128)} async-done(((f32[512,256]{1,0:T(8,128)}), f32[4096,256]{1,0:T(8,128)}) %all-gather.4.cloned.1.call-update) | async-done | bytes 4194320 | tf_op jit(solution)/shard_map/all_gather | solution.py:27
  50.2 0.0 copy-start.1
  50.2 0.0 copy-start.2
  50.2 9.9 %fusion.20 = f32[256,384]{1,0:T(8,128)S(1)} fusion(f32[4096,256]{1,0:T(8,128)} %all-gather.4.cloned.1.call-done, f32[4096,384]{1,0:T(8,128)} %param.5), kind=kOutput, calls=%fused_computation.29 | convolution fusion | flops 4831838208 | bytes 10878976 | tf_op jit(solution)/shard_map/dot_general | solution.py:15
  60.2 0.8 fusion.21
  61.0 0.0 copy-done.1
  61.0 0.0 copy-done.2
  61.0 6.0 %bitcast_subtract_fusion = f32[4096,384]{0,1:T(8,128)S(1)} fusion(f32[4096,384]{0,1:T(8,128)S(1)} %copy-done.1, f32[384,256]{1,0:T(8,128)S(1)} %fusion.21, f32[4096,256]{1,0:T(8,128)S(1)} %copy-done.2), kind=kOutput, calls=%fused_computation.1 | convolution fusion | flops 4833411072 | bytes 17170432 | tf_op jit(solution)/shard_map/dot_general | solution.py:21
  67.0 0.0 copy-start
  67.0 2.7 %copy-done = f32[4096,384]{0,1:T(8,128)} copy-done((f32[4096,384]{0,1:T(8,128)}, f32[4096,384]{0,1:T(8,128)S(1)}, u32[]{:S(2)}) %copy-start) | copy-done | bytes 6291480
  69.8 1.5 collective-permute-start
  71.3 10.8 %all-gather.8.cloned.1.call-done = f32[1024,256]{1,0:T(8,128)} async-done(((f32[256,256]{1,0:T(8,128)}), f32[1024,256]{1,0:T(8,128)}) %all-gather.8.cloned.1.call-update) | async-done | bytes 1048592 | tf_op jit(solution)/shard_map/all_gather | solution.py:39
  82.1 5.2 %collective-permute-done = f32[256,384]{0,1:T(8,128)S(1)} collective-permute-done((f32[256,384]{0,1:T(8,128)S(1)}, f32[256,384]{0,1:T(8,128)S(1)}, u32[]{:S(2)}, u32[]{:S(2)}) %collective-permute-start) | collective-permute-done | bytes 393248 | tf_op jit(solution)/shard_map/ppermute | solution.py:11
  87.3 1.7 %convolution_add_fusion.1 = f32[256,384]{0,1:T(8,128)S(1)} fusion(f32[1024,256]{1,0:T(8,128)} %all-gather.8.cloned.1.call-done, s32[]{:T(128)S(6)} %select_n.79, f32[256,384]{0,1:T(8,128)S(1)} %collective-permute-done, pred[]{:T(512)S(6)} %eq.20, f32[4096,384]{0,1:T(8,128)} %copy-done), kind=kOutput, calls=%fused_computation.7 | convolution fusion | flops 302284800 | bytes 2229760 | tf_op jit(solution)/shard_map/dot_general | solution.py:15
  89.0 26.9 %all-gather.6.cloned.1.call-done = f32[1024,256]{1,0:T(8,128)} async-done(((f32[256,256]{1,0:T(8,128)}), f32[1024,256]{1,0:T(8,128)}) %all-gather.6.cloned.1.call-update) | async-done | bytes 1048592 | tf_op jit(solution)/shard_map/all_gather | solution.py:40
  115.9 2.0 %fusion.4 = f32[256,384]{1,0:T(8,128)S(1)} fusion(f32[256,384]{0,1:T(8,128)S(1)} %convolution_add_fusion.1, f32[1024,256]{1,0:T(8,128)} %all-gather.6.cloned.1.call-done, s32[]{:T(128)S(6)} %select_n.79), kind=kOutput, calls=%fused_computation.11 | convolution fusion | flops 301989888 | bytes 1048580 | tf_op jit(solution)/shard_map/dot_general | solution.py:15
  117.9 0.2 copy.7
  118.0 1.1 fusion.12
  119.1 0.0 copy-start.3
  119.1 1.9 %collective-permute-start.1 = (f32[256,384]{0,1:T(8,128)S(1)}, f32[256,384]{0,1:T(8,128)S(1)}, u32[]{:S(2)}, u32[]{:S(2)}) collective-permute-start(f32[256,384]{0,1:T(8,128)S(1)} %fusion.12), channel_id=1, source_target_pairs={{0,16},{8,24},{16,0},{24,8},{1,17},{9,25},{17,1},{25,9},{2,18},{10... | collective-permute-start | bytes 1179656 | tf_op jit(solution)/shard_map/ppermute | solution.py:11
  121.0 5.6 %slice.9 = f32[3840,384]{0,1:T(8,128)} slice(f32[4096,384]{0,1:T(8,128)} %copy-done), slice={[256:4096], [0:384]} | slice | bytes 11796480 | tf_op jit(solution)/shard_map/slice | solution.py:35
  126.6 0.0 copy-done.3
  126.6 1.8 %fusion = f32[256,384]{0,1:T(8,128)S(1)} fusion(f32[256,384]{1,0:T(8,128)S(1)} %fusion.4, f32[1024,256]{1,0:T(8,128)S(1)} %copy-done.3, s32[]{:T(128)S(6)} %select_n.79, pred[]{:T(512)S(6)} %eq.20, f32[256,384]{0,1:T(8,128)S(1)} %collective-permute-done, f32[4096,384]{0,1:T(8,128)} %copy-done), kind=kOutput, calls=%fused_computation.3 | convolution fusion | flops 302284800 | bytes 1835013 | tf_op jit(solution)/shard_map/dot_general | solution.py:21
  128.4 10.5 %collective-permute-done.1 = f32[256,384]{0,1:T(8,128)S(1)} collective-permute-done((f32[256,384]{0,1:T(8,128)S(1)}, f32[256,384]{0,1:T(8,128)S(1)}, u32[]{:S(2)}, u32[]{:S(2)}) %collective-permute-start.1) | collective-permute-done | bytes 393248 | tf_op jit(solution)/shard_map/ppermute | solution.py:11
  138.9 0.5 convolution_add_fusion
  139.4 2.0 %fusion.2 = f32[256,384]{1,0:T(8,128)S(1)} fusion(f32[256,384]{0,1:T(8,128)S(1)} %convolution_add_fusion, f32[1024,256]{1,0:T(8,128)} %all-gather.6.cloned.1.call-done, s32[]{:T(128)S(6)} %select_n.83), kind=kOutput, calls=%fused_computation.9 | convolution fusion | flops 301989888 | bytes 1048580 | tf_op jit(solution)/shard_map/dot_general | solution.py:15
  141.4 0.2 copy.8
  141.6 0.8 subtract_select_fusion
  142.4 6.0 %pad_maximum_fusion = f32[4096,384]{0,1:T(8,128)} fusion(f32[3840,384]{0,1:T(8,128)} %slice.9, f32[256,384]{0,1:T(8,128)S(1)} %subtract_select_fusion), kind=kLoop, calls=%fused_computation | loop fusion | flops 1572864 | bytes 12582912 | tf_op jit(solution)/shard_map/concatenate | solution.py:61
  148.5 6.6 %copy.11 = f32[4096,384]{1,0:T(8,128)} copy(f32[4096,384]{0,1:T(8,128)} %pad_maximum_fusion) | data formatting | bytes 12582912 | tf_op jit(solution)/shard_map/concatenate | solution.py:61
  (1 shorter events, 0.0 us)
Async XLA Ops:
  6.5 43.7 %all-gather.4.cloned.1.call-start = ((), (), s32[]{:S(2)}) async-start(), calls=%async_computation | async-start | bytes 4718592 | tf_op jit(solution)/shard_map/all_gather | solution.py:27
  7.3 74.9 %all-gather.8.cloned.1.call-start = ((), (), s32[]{:S(2)}) async-start(), calls=%async_computation.2 | async-start | bytes 1310720 | tf_op jit(solution)/shard_map/all_gather | solution.py:39
  19.9 96.0 %all-gather.6.cloned.1.call-start = ((), (), s32[]{:S(2)}) async-start(), calls=%async_computation.1 | async-start | bytes 1310720 | tf_op jit(solution)/shard_map/all_gather | solution.py:40
  50.2 10.7 %copy-start.1 = (f32[4096,384]{0,1:T(8,128)S(1)}, f32[4096,384]{0,1:T(8,128)}, u32[]{:S(2)}) copy-start(f32[4096,384]{0,1:T(8,128)} %copy.6) | copy-start | bytes 18874372
  50.2 10.7 %copy-start.2 = (f32[4096,256]{1,0:T(8,128)S(1)}, f32[4096,256]{1,0:T(8,128)}, u32[]{:S(2)}) copy-start(f32[4096,256]{1,0:T(8,128)} %all-gather.4.cloned.1.call-done) | copy-start | bytes 12582916
  67.0 2.7 %copy-start = (f32[4096,384]{0,1:T(8,128)}, f32[4096,384]{0,1:T(8,128)S(1)}, u32[]{:S(2)}) copy-start(f32[4096,384]{0,1:T(8,128)S(1)} %bitcast_subtract_fusion) | copy-start | bytes 18874372
  69.8 17.5 %collective-permute-start = (f32[256,384]{0,1:T(8,128)S(1)}, f32[256,384]{0,1:T(8,128)S(1)}, u32[]{:S(2)}, u32[]{:S(2)}) collective-permute-start(f32[256,384]{0,1:T(8,128)S(1)} %slice.8), channel_id=1, source_target_pairs={{0,8},{8,0},{16,24},{24,16},{1,9},{9,1},{17,25},{25,17},{2,10},{10... | collective-permute-start | bytes 1179656 | tf_op jit(solution)/shard_map/ppermute | solution.py:11
  119.1 7.4 %copy-start.3 = (f32[1024,256]{1,0:T(8,128)S(1)}, f32[1024,256]{1,0:T(8,128)}, u32[]{:S(2)}) copy-start(f32[1024,256]{1,0:T(8,128)} %all-gather.8.cloned.1.call-done) | copy-start | bytes 3145732
  119.1 19.8 %collective-permute-start.1 = (f32[256,384]{0,1:T(8,128)S(1)}, f32[256,384]{0,1:T(8,128)S(1)}, u32[]{:S(2)}, u32[]{:S(2)}) collective-permute-start(f32[256,384]{0,1:T(8,128)S(1)} %fusion.12), channel_id=1, source_target_pairs={{0,16},{8,24},{16,0},{24,8},{1,17},{9,25},{17,1},{25,9},{2,18},{10... | collective-permute-start | bytes 1179656 | tf_op jit(solution)/shard_map/ppermute | solution.py:11
Sparse Core Ops, SparseCore 0:
  9.2 40.9 all-gather.3
  51.8 30.2 all-gather.7
  83.7 32.1 all-gather.5
where the time goes:
time: 162 us
  waiting for transfers between devices  57.4 us (35%)
  blocking collectives  33 us (20%)
  matrix products  25.5 us (16%)
  local copies, waits for them, and re-layouts  21.8 us (13%)
  between operations  13.2 us (8%)
  other arithmetic  7.11 us (4%)
  starting transfers between devices  3.49 us (2%)
    all_gather x1, waiting for transfers between devices, shards(): lax.all_gather(own_factor, 'row', axis=0, tiled=True)  26.9 us
    dot_general x6, matrix products, left_product(): lax.dot_general(first, second, contract_rows, precision=highest, preferre...  16.9 us
    ppermute x2, waiting for transfers between devices, swapped(): lax.ppermute(array, axis, [(i, i ^ 1 << apart) for i in range(lax.axis_si...  15.7 us
    all_gather x1, blocking collectives, shards(): lax.all_gather(tree_vectors, 'col', axis=0, tiled=True)  12.6 us
    all_gather x1, waiting for transfers between devices, shards(): lax.all_gather(own_vectors, 'row', axis=0, tiled=True)  10.8 us
    all_gather x1, blocking collectives, shards(): lax.all_gather(tree_factor, 'col', axis=0, tiled=True)  10.6 us
    all_gather x1, blocking collectives, shards(): lax.all_gather(leaf_factor, 'col', axis=0, tiled=True)  9.82 us
    unnamed x9, local copies, waits for them, and re-layouts  9.34 us
  transfers between devices with their start and end apart: 5, of which 5 were waited for; matrix products, arithmetic and copies ran while one was open for 20% of the time, Pallas kernels for 0%

commit v1 on v0

--- a/solution.py
+++ b/solution.py
@@ -5,6 +5,32 @@
 
 highest = lax.Precision.HIGHEST
 contract_rows = (((0,), (0,)), ((), ()))
+
+
+def update_loops(arr_in, dim_at):
+    arr_in = jnp.moveaxis(arr_in, 0, dim_at)
+    value_now = arr_in.shape
+    return arr_in.reshape(
+        *value_now[:dim_at], value_now[dim_at] * value_now[dim_at + 1], *value_now[dim_at + 2 :]
+    )
+
+
+def remake_sheets_for(load, mesh_ax):
+    mixed_arr = load[None]
+    shares = lax.axis_size(mesh_ax)
+    for hop_no in range(shares.bit_length() - 1):
+        f_now = 1 << hop_no
+        b_now = lax.ppermute(mixed_arr, mesh_ax, [(jj, jj ^ f_now) for jj in range(shares)])
+        heard = jnp.stack([mixed_arr, b_now])
+        n_now = lax.axis_index(mesh_ax)
+        state_next = n_now >> hop_no & 1
+        mixed_arr = jnp.where(state_next == 0, heard, heard[::-1]).reshape(-1, *load.shape)
+    return mixed_arr
+
+
+def measure_packet(target, x_in, at_axis):
+    arr_out = remake_sheets_for(target, x_in)
+    return update_loops(arr_out, at_axis)
 
 
 def swapped(array, axis, apart):
@@ -37,7 +63,7 @@
     position = lax.axis_index("row")
     pair_vectors, pair_factor = (
         lax.all_gather(own_vectors, "row", axis=0, tiled=True),
-        lax.all_gather(own_factor, "row", axis=0, tiled=True),
+        measure_packet(own_factor, "row", 0),
     )
     current = upper_rows
     final_top = upper_rows

time: 162 us -> 146 us (0.901)
  waiting for transfers between devices: 57.4 us -> 38.1 us
  starting transfers between devices: 3.49 us -> 6.16 us
    all_gather x1 -> x0, waiting for transfers between devices: 26.9 us -> none  [shards(): lax.all_gather(own_factor, 'row', axis=0, tiled=True)]
    ppermute x0 -> x2, waiting for transfers between devices: none -> 17.4 us  [remake_sheets_for(): lax.ppermute(mixed_arr, mesh_ax, [(jj, jj ^ f_now) for jj in range(shares)])]
    all_gather x1, waiting for transfers between devices: 10.8 us -> 2.01 us  [shards(): lax.all_gather(own_vectors, 'row', axis=0, tiled=True)]
    ppermute x0 -> x2, starting transfers between devices: none -> 4.06 us  [remake_sheets_for(): lax.ppermute(mixed_arr, mesh_ax, [(jj, jj ^ f_now) for jj in range(shares)])]
    dot_general x3, matrix products: 8.63 us -> 11.7 us  [plain_product(): jnp.dot(first, second, precision=highest, preferred_element_type=jnp.floa...]
    all_gather x1, waiting for transfers between devices: 3.21 us -> 0.35 us  [shards(): lax.all_gather(leaf_vectors, 'col', axis=0, tiled=True)]
    all_gather x1, blocking collectives: 12.6 us -> 10.5 us  [shards(): lax.all_gather(tree_vectors, 'col', axis=0, tiled=True)]
    dot_general x6, matrix products: 16.9 us -> 14.8 us  [left_product(): lax.dot_general(first, second, contract_rows, precision=highest, preferre...]
  transfers between devices with their start and end apart: 5 -> 6, of which waited for: 5 -> 5; matrix products, arithmetic and copies ran while one was open for 20% -> 23% of each run, Pallas kernels for 0% -> 0%
where the time goes in v1:
time: 146 us
  waiting for transfers between devices  38.1 us (26%)
  blocking collectives  31.7 us (22%)
  matrix products  26.5 us (18%)
  local copies, waits for them, and re-layouts  22.3 us (15%)
  between operations  13.6 us (9%)
  other arithmetic  7.4 us (5%)
  starting transfers between devices  6.16 us (4%)
    ppermute x2, waiting for transfers between devices, swapped(): lax.ppermute(array, axis, [(i, i ^ 1 << apart) for i in range(lax.axis_si...  17.6 us
    ppermute x2, waiting for transfers between devices, remake_sheets_for(): lax.ppermute(mixed_arr, mesh_ax, [(jj, jj ^ f_now) for jj in range(shares)])  17.4 us
    dot_general x6, matrix products, left_product(): lax.dot_general(first, second, contract_rows, precision=highest, preferre...  14.8 us
    dot_general x3, matrix products, plain_product(): jnp.dot(first, second, precision=highest, preferred_element_type=jnp.floa...  11.7 us
    all_gather x1, blocking collectives, shards(): lax.all_gather(tree_factor, 'col', axis=0, tiled=True)  11 us
    all_gather x1, blocking collectives, shards(): lax.all_gather(tree_vectors, 'col', axis=0, tiled=True)  10.5 us
    all_gather x1, blocking collectives, shards(): lax.all_gather(leaf_factor, 'col', axis=0, tiled=True)  10.2 us
    unnamed x9, local copies, waits for them, and re-layouts  9.72 us
  transfers between devices with their start and end apart: 6, of which 5 were waited for; matrix products, arithmetic and copies ran while one was open for 23% of the time, Pallas kernels for 0%

profile of v1, /device:TPU:0, one launch (start us, length us, event | category | flops | bytes accessed | tf_op | source)
XLA Modules:
  0.0 145.8 jit_solution(5518111521581944324)
XLA Ops:
  6.5 0.0 all-gather.3.cloned.1.call-start
  6.5 0.7 all-gather.3.cloned.1.call-update
  7.3 0.0 all-gather.5.cloned.1.call-start
  7.3 11.0 %all_gather.17 = f32[256,256]{1,0:T(8,128)S(1)} all-gather(f32[32,256]{1,0:T(8,128)} %param.9), channel_id=1, replica_groups=mesh['row'=4,'col'=8] {'col'}, dimensions={0}, use_global_device_ids=true | all-gather | bytes 294912 | tf_op jit(solution)/shard_map/all_gather | solution.py:56
  18.3 1.6 %collective-permute-start.1 = (f32[1,256,256]{2,1,0:T(8,128)S(1)}, f32[1,256,256]{2,1,0:T(8,128)S(1)}, u32[]{:S(2)}, u32[]{:S(2)}) collective-permute-start(f32[1,256,256]{2,1,0:T(8,128)S(1)} %bitcast.23), channel_id=1, source_target_pairs={{0,8},{8,0},{16,24},{24,16},{1,9},{9,1},{17,25},{25,17},{2,10},{10... | collective-permute-start | bytes 786440 | tf_op jit(solution)/shard_map/ppermute | solution.py:23
  19.9 10.5 %all_gather.18 = f32[256,256]{1,0:T(8,128)} all-gather(f32[32,256]{1,0:T(8,128)} %param.8), channel_id=1, replica_groups=mesh['row'=4,'col'=8] {'col'}, dimensions={0}, use_global_device_ids=true | all-gather | bytes 294912 | tf_op jit(solution)/shard_map/all_gather | solution.py:55
  30.4 0.0 all-gather.5.cloned.1.call-update
  30.4 0.0 copy-start.3
  30.5 7.0 %copy.6 = f32[4096,384]{0,1:T(8,128)} copy(f32[4096,384]{1,0:T(8,128)} %param.5) | data formatting | bytes 12582912 | tf_op args[0]
  37.5 0.0 copy-done.3
  37.5 10.2 %all_gather.16 = f32[256,256]{1,0:T(8,128)S(1)} all-gather(f32[32,256]{1,0:T(8,128)S(1)} %copy-done.3), channel_id=1, replica_groups=mesh['row'=4,'col'=8] {'col'}, dimensions={0}, use_global_device_ids=true | all-gather | bytes 294912 | tf_op jit(solution)/shard_map/all_gather | solution.py:54
  47.7 0.0 collective-permute-done.1
  47.7 0.1 fusion.3
  47.8 2.5 %collective-permute-start.2 = (f32[2,256,256]{2,1,0:T(8,128)S(1)}, f32[2,256,256]{2,1,0:T(8,128)S(1)}, u32[]{:S(2)}, u32[]{:S(2)}) collective-permute-start(f32[2,256,256]{2,1,0:T(8,128)S(1)} %get-tuple-element.6), channel_id=1, source_target_pairs={{0,16},{8,24},{16,0},{24,8},{1,17},{9,25},{17,1},{25,9},{2,18},{10... | collective-permute-start | bytes 1572872 | tf_op jit(solution)/shard_map/ppermute | solution.py:23
  50.3 0.4 all-gather.3.cloned.1.call-done
  50.7 0.0 copy-start.1
  50.7 9.7 %fusion.22 = f32[256,384]{1,0:T(8,128)S(1)} fusion(f32[4096,256]{1,0:T(8,128)} %all-gather.3.cloned.1.call-done, f32[4096,384]{1,0:T(8,128)} %param.5), kind=kOutput, calls=%fused_computation.35 | convolution fusion | flops 4831838208 | bytes 10878976 | tf_op jit(solution)/shard_map/dot_general | solution.py:41
  60.4 0.8 fusion.23
  61.2 0.0 copy-done.1
  61.2 8.1 %bitcast_subtract_fusion = f32[4096,384]{0,1:T(8,128)S(1)} fusion(f32[4096,384]{0,1:T(8,128)} %copy.6, f32[384,256]{1,0:T(8,128)S(1)} %fusion.23, f32[4096,256]{1,0:T(8,128)S(1)} %copy-done.1), kind=kOutput, calls=%fused_computation.1 | convolution fusion | flops 4833411072 | bytes 17170432 | tf_op jit(solution)/shard_map/dot_general | solution.py:47
  69.3 0.0 copy-start
  69.3 2.7 %copy-done = f32[4096,384]{0,1:T(8,128)} copy-done((f32[4096,384]{0,1:T(8,128)}, f32[4096,384]{0,1:T(8,128)S(1)}, u32[]{:S(2)}) %copy-start) | copy-done | bytes 6291480
  72.1 1.6 %collective-permute-start = (f32[256,384]{0,1:T(8,128)S(1)}, f32[256,384]{0,1:T(8,128)S(1)}, u32[]{:S(2)}, u32[]{:S(2)}) collective-permute-start(f32[256,384]{0,1:T(8,128)S(1)} %slice.8), channel_id=1, source_target_pairs={{0,8},{8,0},{16,24},{24,16},{1,9},{9,1},{17,25},{25,17},{2,10},{10... | collective-permute-start | bytes 1179656 | tf_op jit(solution)/shard_map/ppermute | solution.py:37
  73.6 17.4 %collective-permute-done.2 = f32[2,256,256]{2,1,0:T(8,128)S(1)} collective-permute-done((f32[2,256,256]{2,1,0:T(8,128)S(1)}, f32[2,256,256]{2,1,0:T(8,128)S(1)}, u32[]{:S(2)}, u32[]{:S(2)}) %collective-permute-start.2) | collective-permute-done | bytes 524320 | tf_op jit(solution)/shard_map/ppermute | solution.py:23
  91.0 0.1 pad_maximum_fusion.1
  91.1 0.1 reverse_select_fusion
  91.2 2.0 %all-gather.5.cloned.1.call-done = f32[1024,256]{1,0:T(8,128)} async-done(((f32[256,256]{1,0:T(8,128)}), f32[1024,256]{1,0:T(8,128)}) %all-gather.5.cloned.1.call-update) | async-done | bytes 1048592 | tf_op jit(solution)/shard_map/all_gather | solution.py:65
  93.2 5.3 %collective-permute-done = f32[256,384]{0,1:T(8,128)S(1)} collective-permute-done((f32[256,384]{0,1:T(8,128)S(1)}, f32[256,384]{0,1:T(8,128)S(1)}, u32[]{:S(2)}, u32[]{:S(2)}) %collective-permute-start) | collective-permute-done | bytes 393248 | tf_op jit(solution)/shard_map/ppermute | solution.py:37
  98.5 1.7 %convolution_add_fusion.1 = f32[256,384]{0,1:T(8,128)S(1)} fusion(f32[1024,256]{1,0:T(8,128)} %all-gather.5.cloned.1.call-done, s32[]{:T(128)S(6)} %select_n.99, f32[256,384]{0,1:T(8,128)S(1)} %collective-permute-done, pred[]{:T(512)S(6)} %eq.26, f32[4096,384]{0,1:T(8,128)} %copy-done), kind=kOutput, calls=%fused_computation.8 | convolution fusion | flops 302284800 | bytes 2229760 | tf_op jit(solution)/shard_map/dot_general | solution.py:41
  100.2 1.1 fusion.6
  101.3 0.2 copy.7
  101.5 1.1 fusion.14
  102.6 0.5 collective-permute-start.3
  103.1 0.0 copy-start.2
  103.1 5.7 %slice.9 = f32[3840,384]{0,1:T(8,128)} slice(f32[4096,384]{0,1:T(8,128)} %copy-done), slice={[256:4096], [0:384]} | slice | bytes 11796480 | tf_op jit(solution)/shard_map/slice | solution.py:61
  108.7 0.0 copy-done.2
  108.7 1.8 %fusion = f32[256,384]{0,1:T(8,128)S(1)} fusion(f32[256,384]{1,0:T(8,128)S(1)} %fusion.6, f32[1024,256]{1,0:T(8,128)S(1)} %copy-done.2, s32[]{:T(128)S(6)} %select_n.99, pred[]{:T(512)S(6)} %eq.26, f32[256,384]{0,1:T(8,128)S(1)} %collective-permute-done, f32[4096,384]{0,1:T(8,128)} %copy-done), kind=kOutput, calls=%fused_computation.4 | convolution fusion | flops 302284800 | bytes 1835013 | tf_op jit(solution)/shard_map/dot_general | solution.py:47
  110.5 12.3 %collective-permute-done.3 = f32[256,384]{0,1:T(8,128)S(1)} collective-permute-done((f32[256,384]{0,1:T(8,128)S(1)}, f32[256,384]{0,1:T(8,128)S(1)}, u32[]{:S(2)}, u32[]{:S(2)}) %collective-permute-start.3) | collective-permute-done | bytes 393248 | tf_op jit(solution)/shard_map/ppermute | solution.py:37
  122.8 0.5 convolution_add_fusion
  123.3 1.1 fusion.4
  124.4 0.2 copy.8
  124.6 1.8 %subtract_select_fusion = f32[256,384]{0,1:T(8,128)S(1)} fusion(f32[256,384]{0,1:T(8,128)S(1)} %copy.8, f32[256,384]{0,1:T(8,128)S(1)} %fusion, f32[256,384]{1,0:T(8,128)S(1)} %fusion.4, f32[1024,256]{1,0:T(8,128)} %all-gather.5.cloned.1.call-done, s32[]{:T(128)S(6)} %select_n.103, pred[]{:T(512)S(6)} %eq.29, pred[]{:T(512)S(6)} %eq.24, ...), kind=kOutput, calls=%fused_computation.14 | convolution fusion | flops 302579712 | bytes 2621447 | tf_op jit(solution)/shard_map/dot_general | solution.py:47
  126.3 6.0 %pad_maximum_fusion = f32[4096,384]{0,1:T(8,128)} fusion(f32[3840,384]{0,1:T(8,128)} %slice.9, f32[256,384]{0,1:T(8,128)S(1)} %subtract_select_fusion), kind=kLoop, calls=%fused_computation | loop fusion | flops 1572864 | bytes 12582912 | tf_op jit(solution)/shard_map/concatenate | solution.py:87
  132.4 6.6 %copy.11 = f32[4096,384]{1,0:T(8,128)} copy(f32[4096,384]{0,1:T(8,128)} %pad_maximum_fusion) | data formatting | bytes 12582912 | tf_op jit(solution)/shard_map/concatenate | solution.py:87
  (2 shorter events, 0.1 us)
Async XLA Ops:
  6.5 44.1 %all-gather.3.cloned.1.call-start = ((), (), s32[]{:S(2)}) async-start(), calls=%async_computation | async-start | bytes 4718592 | tf_op jit(solution)/shard_map/all_gather | solution.py:53
  7.3 86.0 %all-gather.5.cloned.1.call-start = ((), (), s32[]{:S(2)}) async-start(), calls=%async_computation.1 | async-start | bytes 1310720 | tf_op jit(solution)/shard_map/all_gather | solution.py:65
  18.3 29.4 %collective-permute-start.1 = (f32[1,256,256]{2,1,0:T(8,128)S(1)}, f32[1,256,256]{2,1,0:T(8,128)S(1)}, u32[]{:S(2)}, u32[]{:S(2)}) collective-permute-start(f32[1,256,256]{2,1,0:T(8,128)S(1)} %bitcast.23), channel_id=1, source_target_pairs={{0,8},{8,0},{16,24},{24,16},{1,9},{9,1},{17,25},{25,17},{2,10},{10... | collective-permute-start | bytes 786440 | tf_op jit(solution)/shard_map/ppermute | solution.py:23
  30.4 7.0 %copy-start.3 = (f32[32,256]{1,0:T(8,128)S(1)}, f32[32,256]{1,0:T(8,128)}, u32[]{:S(2)}) copy-start(f32[32,256]{1,0:T(8,128)} %param.7) | copy-start | bytes 98308
  47.8 43.2 %collective-permute-start.2 = (f32[2,256,256]{2,1,0:T(8,128)S(1)}, f32[2,256,256]{2,1,0:T(8,128)S(1)}, u32[]{:S(2)}, u32[]{:S(2)}) collective-permute-start(f32[2,256,256]{2,1,0:T(8,128)S(1)} %get-tuple-element.6), channel_id=1, source_target_pairs={{0,16},{8,24},{16,0},{24,8},{1,17},{9,25},{17,1},{25,9},{2,18},{10... | collective-permute-start | bytes 1572872 | tf_op jit(solution)/shard_map/ppermute | solution.py:23
  50.7 10.5 %copy-start.1 = (f32[4096,256]{1,0:T(8,128)S(1)}, f32[4096,256]{1,0:T(8,128)}, u32[]{:S(2)}) copy-start(f32[4096,256]{1,0:T(8,128)} %all-gather.3.cloned.1.call-done) | copy-start | bytes 12582916
  69.3 2.7 %copy-start = (f32[4096,384]{0,1:T(8,128)}, f32[4096,384]{0,1:T(8,128)S(1)}, u32[]{:S(2)}) copy-start(f32[4096,384]{0,1:T(8,128)S(1)} %bitcast_subtract_fusion) | copy-start | bytes 18874372
  72.1 26.5 %collective-permute-start = (f32[256,384]{0,1:T(8,128)S(1)}, f32[256,384]{0,1:T(8,128)S(1)}, u32[]{:S(2)}, u32[]{:S(2)}) collective-permute-start(f32[256,384]{0,1:T(8,128)S(1)} %slice.8), channel_id=1, source_target_pairs={{0,8},{8,0},{16,24},{24,16},{1,9},{9,1},{17,25},{25,17},{2,10},{10... | collective-permute-start | bytes 1179656 | tf_op jit(solution)/shard_map/ppermute | solution.py:37
  102.6 20.3 %collective-permute-start.3 = (f32[256,384]{0,1:T(8,128)S(1)}, f32[256,384]{0,1:T(8,128)S(1)}, u32[]{:S(2)}, u32[]{:S(2)}) collective-permute-start(f32[256,384]{0,1:T(8,128)S(1)} %fusion.14), channel_id=1, source_target_pairs={{0,16},{8,24},{16,0},{24,8},{1,17},{9,25},{17,1},{25,9},{2,18},{10... | collective-permute-start | bytes 1179656 | tf_op jit(solution)/shard_map/ppermute | solution.py:37
  103.1 5.7 %copy-start.2 = (f32[1024,256]{1,0:T(8,128)S(1)}, f32[1024,256]{1,0:T(8,128)}, u32[]{:S(2)}) copy-start(f32[1024,256]{1,0:T(8,128)} %all-gather.5.cloned.1.call-done) | copy-start | bytes 3145732
Sparse Core Ops, SparseCore 0:
  9.2 41.4 all-gather.2
  52.2 40.9 all-gather.4
